TPU v7x, 256 devices: a whole 4x4x8 slice. The times are simulated.
256 devices in a mesh: sub: 32 (over z, x), agg: 8 (over y, core).
Axes of the slice: x: 4, y: 4, z: 8, core: 2. Of those that a mesh axis runs over, the one named last changes fastest.
Arguments:
- dual_load: float32 [8, 32, 64, 1536], P('agg', 'sub'), may hold values from -58 to 58
- interface_inverse: bfloat16 [8, 32, 1536, 1536], P('agg', 'sub'), may hold values from -1 to 2.5, as said below
- dirichlet: bfloat16 [8, 32, 1536, 1536], P('agg', 'sub'), may hold values from -1 to 2.5, as said below
- coupling: bfloat16 [8, 32, 128, 1536], P('agg', 'sub'), may hold values from -0.15625 to 0.15625
- neighbours: int32 [8, 32, 8], P('agg', 'sub'), may hold values from -1 to 31, as said below
- face_counts: int32 [8, 32, 8], P('agg', 'sub'), may hold values from 0 to 192, as said below
- owners: int32 [8, 32, 128, 1], P('agg', 'sub'), may hold values from 0 to 7; in each aligned block of 128 rows (0 to 127, 128 to 255, ..., all dimensions but the last counted through in order) at most 48 rows name the same one
- primal_rows: int32 [8, 32, 128], P('agg', 'sub'), may hold values from 0 to 1023
- coarse_inverse: float32 [8, 1024, 1024], P('agg', 'sub'), may hold values from -1 to 1.5, as said below
Outputs:
- solution: float32 [8, 32, 64, 1536], P('agg', 'sub')
- residual: float32 [8, 32, 64, 1536], P('agg', 'sub')
Inputs may be any that keep to these rules, and one draw needn't show every extreme that they name: `neighbours`: each subdomain lists peers of its own aggregate by their index along sub, -1 in empty slots; no peer twice; if j lists i then i lists j; every listed peer lies within a cyclic distance of 4 along sub. `face_counts`: 0 exactly in empty slots, 48 or more elsewhere; both sides of a face give the same count and hold its rows in the same order. `owners`: among the 128 primal rows of one subdomain no aggregate is named more than 48 times. `interface_inverse`: each subdomain's matrix is symmetric positive definite. `dirichlet`: each subdomain's matrix is symmetric positive definite. `coarse_inverse`: each aggregate's matrix is symmetric positive definite.
All inputs are finite; a program needn't handle non-finite values.
Results may differ from a plain program's by a relative error of at most 0.011.
Values sent between devices are 32-bit elements; how exact they have to be, the bound alone decides.
No kernel may reach another device: no remote copies, remote signals or barrier semaphores. Data moves between devices by JAX's collectives and lax.ppermute only.
A program may use at most 128 MiB of HBM per device.

v0:
```python
import jax
import jax.numpy as jnp
from jax import lax
from jax.sharding import PartitionSpec as P

NC = 1024
CAP = 48
ITERS = 2
FULL_PRECISION = lax.Precision.HIGHEST
CONTRACT_LAST = (((1,), (1,)), ((), ()))


def from_behind_2(block, axis, distance):
    devices = range(lax.axis_size(axis))
    route = [((i - distance) % len(devices), i) for i in devices]
    return lax.ppermute(block, axis, route)


def shards(
    dual_load,
    interface_inverse,
    dirichlet,
    coupling,
    neighbours,
    face_counts,
    owners,
    primal_rows,
    coarse_inverse,
):
    inverse_block = interface_inverse[0, 0]
    dirichlet_block = dirichlet[0, 0]
    coupling_block = coupling[0, 0]
    peer_list = neighbours[0, 0]
    count_list = face_counts[0, 0]
    sub_count = lax.axis_size("sub")
    agg_count = lax.axis_size("agg")
    position = lax.axis_index("sub")
    slot_count = peer_list.shape[0]
    inner_order = inverse_block.shape[0]
    face_depth = inner_order // slot_count
    reach = min(4, (sub_count - 1) // 2)
    inside = (
        (jnp.arange(face_depth, dtype=jnp.int32)[None, :] < count_list[:, None])
        .reshape(1, inner_order)
        .astype(jnp.float32)
    )

    def assemble(local):
        case_count = local.shape[0]
        faces = local.reshape(case_count, slot_count, face_depth)
        placed = jnp.zeros_like(faces)
        for distance in range(1, reach + 1):
            ahead = (position + distance) % sub_count
            behind = (position + sub_count - distance) % sub_count
            to_ahead = (peer_list == ahead).astype(jnp.float32)[None, :, None]
            to_behind = (peer_list == behind).astype(jnp.float32)[None, :, None]
            upward = jnp.sum(faces * to_ahead, axis=1)
            downward = jnp.sum(faces * to_behind, axis=1)
            from_behind = from_behind_2(upward, "sub", distance)
            from_ahead = from_behind_2(downward, "sub", -distance)
            placed = (
                placed + to_behind * from_behind[:, None, :] + to_ahead * from_ahead[:, None, :]
            )
        return inside * (local + placed.reshape(case_count, inner_order))

    owner_ids = owners[0, 0, :, 0]
    row_ids = primal_rows[0, 0]
    owner_hot = (owner_ids[:, None] == jnp.arange(agg_count, dtype=jnp.int32)[None, :]).astype(
        jnp.int32
    )
    earlier = jnp.cumsum(owner_hot, axis=0) - owner_hot
    owner_rank = jnp.sum(earlier * owner_hot, axis=1)
    slot_index = owner_ids * CAP + owner_rank
    packing = slot_index[:, None] == jnp.arange(agg_count * CAP, dtype=jnp.int32)[None, :]
    packing_float = packing.astype(jnp.float32)
    sent_rows = jnp.sum(packing.astype(jnp.int32) * (row_ids[:, None] + 1), axis=0) - 1
    got_rows = lax.all_to_all(sent_rows, "agg", split_axis=0, concat_axis=0, tiled=True)
    scatter_hot = (got_rows[:, None] == jnp.arange(NC, dtype=jnp.int32)[None, :]).astype(
        jnp.float32
    )
    inverse_rows = coarse_inverse[0]

    def precondition(field):
        packed = field.astype(jnp.bfloat16)
        return assemble(
            inside * jnp.dot(packed, dirichlet_block, preferred_element_type=jnp.float32)
        )

    def residual_norm(first, second):
        return lax.psum(jnp.sum(first * second, axis=1), ("sub", "agg"))

    rhs = assemble(inside * dual_load[0, 0])
    solution = jnp.zeros_like(rhs)
    residual = rhs
    precond = precondition(residual)
    direction = precond
    residual_dot = residual_norm(residual, precond)
    for iteration in range(ITERS):
        operator_packed = direction.astype(jnp.bfloat16)
        own = jnp.dot(operator_packed, inverse_block, preferred_element_type=jnp.float32)
        terms = lax.dot_general(
            operator_packed, coupling_block, CONTRACT_LAST, preferred_element_type=jnp.float32
        )
        outgoing = jnp.dot(terms, packing_float, precision=FULL_PRECISION)
        gathered = jnp.dot(
            lax.all_to_all(outgoing, "agg", split_axis=1, concat_axis=1, tiled=True),
            scatter_hot,
            precision=FULL_PRECISION,
        )
        coarse_rhs = lax.psum(gathered, "sub")
        partial_rows = lax.dot_general(
            coarse_rhs, inverse_rows, CONTRACT_LAST, precision=FULL_PRECISION
        )
        coarse_sol = lax.all_gather(partial_rows, "sub", axis=1, tiled=True)
        answer = lax.dot_general(coarse_sol, scatter_hot, CONTRACT_LAST, precision=FULL_PRECISION)
        returned = lax.all_to_all(answer, "agg", split_axis=1, concat_axis=1, tiled=True)
        local_back = lax.dot_general(
            returned, packing_float, CONTRACT_LAST, precision=FULL_PRECISION
        )
        correction = jnp.dot(
            local_back.astype(jnp.bfloat16), coupling_block, preferred_element_type=jnp.float32
        )
        image = assemble(inside * (own + correction))
        alpha = (residual_dot / lax.psum(jnp.sum(direction * image, axis=1), ("sub", "agg")))[
            :, None
        ]
        solution = solution + alpha * direction
        residual = residual - alpha * image
        if iteration + 1 < ITERS:
            precond = precondition(residual)
            next_dot = residual_norm(residual, precond)
            direction = precond + (next_dot / residual_dot)[:, None] * direction
            residual_dot = next_dot
    return (solution[None, None], residual[None, None])


def solution(mesh):
    in_specs = (
        P("agg", "sub", None, None),
        P("agg", "sub", None, None),
        P("agg", "sub", None, None),
        P("agg", "sub", None, None),
        P("agg", "sub", None),
        P("agg", "sub", None),
        P("agg", "sub", None, None),
        P("agg", "sub", None),
        P("agg", "sub", None),
    )
    out_specs = (P("agg", "sub", None, None), P("agg", "sub", None, None))
    return jax.shard_map(shards, mesh=mesh, in_specs=in_specs, out_specs=out_specs, check_vma=False)
```

profile of v0, /device:TPU:1, one launch (start us, length us, event | category | flops | bytes accessed | tf_op | source)
XLA Modules:
  0.0 917.8 jit_solution(6425770265424465426)
XLA Ops:
  13.6 6.6 collective-permute-start.1
  50.8 5.2 fusion.8
  60.5 4.7 collective-permute-start.11
  76.5 10.1 %all-to-all-start.1 = ((s32[8,48,1]{1,2,0:T(1,128)}), s32[8,48,1]{1,2,0:T(1,128)}, u32[]{:S(2)}, u32[]{:S(2)}) async-start(s32[8,48,1]{1,2,0:T(1,128)} %bitcast.111), calls=%async_computation.1 | async-start | bytes 8192 | tf_op jit(solution)/shard_map/all_to_all | solution.py:77
  119.4 4.8 all-to-all-start
  136.4 138.3 %all-reduce.4.cloned.1.call-done = f32[64,1024]{1,0:T(8,128)} async-done(((f32[64,1024]{1,0:T(8,128)}), f32[64,1024]{1,0:T(8,128)}) %all-reduce.4.cloned.1.call-update) | async-done | bytes 262160 | tf_op jit(solution)/shard_map/psum | solution.py:110
  275.9 35.9 %all_gather.6 = f32[64,1024]{0,1:T(8,128)S(1)} all-gather(f32[64,32]{0,1:T(8,128)S(1)} %fusion.58), channel_id=1, replica_groups=mesh['sub'=32,'agg'=8] {'sub'}, dimensions={1}, use_global_device_ids=true | all-gather | bytes 270336 | tf_op jit(solution)/shard_map/all_gather | solution.py:114
  315.8 26.7 %all_to_all.54 = f32[8,1,3072]{2,1,0:T(1,128)} all-to-all(f32[8,1,3072]{2,1,0:T(1,128)} %reshape.670), channel_id=1, replica_groups=mesh['sub'=32,'agg'=8] {'agg'}, dimensions={0} | all-to-all | bytes 196608 | tf_op jit(solution)/shard_map/all_to_all | solution.py:116
  348.1 4.0 fusion.23
  360.2 4.5 collective-permute-start.17
  364.7 3.8 collective-permute-start.21
  394.4 3.9 multiply_reduce_fusion.42
  398.5 77.6 %all-reduce = (f32[64]{0:T(128)S(1)}, f32[64]{0:T(128)S(1)}) all-reduce(f32[64]{0:T(128)S(1)} %get-tuple-element.43, f32[64]{0:T(128)S(1)} %get-tuple-element.42), channel_id=1, replica_groups=mesh['sub'=32,'agg'=8] {'sub','agg'}, use_global_device_ids=true, to_apply=%region_17.18 | all-reduce | flops 128 | bytes 1024 | tf_op jit(solution)/shard_map/psum | solution.py:90
  477.2 3.3 fusion.11
  488.2 3.5 collective-permute-start.29
  505.9 77.6 %psum.45 = f32[64]{0:T(128)S(1)} all-reduce(f32[64]{0:T(128)S(1)} %get-tuple-element.48), channel_id=1, replica_groups=mesh['sub'=32,'agg'=8] {'sub','agg'}, use_global_device_ids=true, to_apply=%region_41.42 | all-reduce | flops 64 | bytes 512 | tf_op jit(solution)/shard_map/psum | solution.py:90
  585.7 8.1 all_to_all.55
  596.3 136.3 %all-reduce.6.cloned.1.call-done = f32[64,1024]{1,0:T(8,128)} async-done(((f32[64,1024]{1,0:T(8,128)}), f32[64,1024]{1,0:T(8,128)}) %all-reduce.6.cloned.1.call-update) | async-done | bytes 262160 | tf_op jit(solution)/shard_map/psum | solution.py:110
  733.9 35.9 %all_gather.7 = f32[64,1024]{0,1:T(8,128)S(1)} all-gather(f32[64,32]{0,1:T(8,128)S(1)} %fusion.56), channel_id=1, replica_groups=mesh['sub'=32,'agg'=8] {'sub'}, dimensions={1}, use_global_device_ids=true | all-gather | bytes 270336 | tf_op jit(solution)/shard_map/all_gather | solution.py:114
  770.8 26.7 %all_to_all.56 = f32[8,1,3072]{2,1,0:T(1,128)S(1)} all-to-all(f32[8,1,3072]{2,1,0:T(1,128)S(1)} %reshape.674), channel_id=1, replica_groups=mesh['sub'=32,'agg'=8] {'agg'}, dimensions={0} | all-to-all | bytes 196608 | tf_op jit(solution)/shard_map/all_to_all | solution.py:116
  799.1 3.3 fusion.20
  807.2 4.5 collective-permute-start.33
  811.7 3.6 collective-permute-start.37
  831.3 77.7 %psum.47 = f32[64]{0:T(128)S(1)} all-reduce(f32[64]{0:T(128)S(1)} %get-tuple-element.46), channel_id=1, replica_groups=mesh['sub'=32,'agg'=8] {'sub','agg'}, use_global_device_ids=true, to_apply=%region_52.53 | all-reduce | flops 64 | bytes 512 | tf_op jit(solution)/shard_map/psum | solution.py:124
  (355 shorter events, 195.7 us)
Async XLA Ops:
  11.5 35.6 %collective-permute-start = (f32[64,192]{1,0:T(8,128)S(1)}, f32[64,192]{1,0:T(8,128)}, u32[]{:S(2)}, u32[]{:S(2)}) collective-permute-start(f32[64,192]{1,0:T(8,128)S(1)} %get-tuple-element.2), channel_id=1, source_target_pairs={{248,0},{0,8},{8,16},{16,24},{24,32},{32,40},{40,48},{48,56},{56,6... | collective-permute-start | bytes 147464 | tf_op jit(solution)/shard_map/ppermute | solution.py:16
  13.6 29.9 %collective-permute-start.1 = (f32[64,192]{1,0:T(8,128)}, f32[64,192]{1,0:T(8,128)}, u32[]{:S(2)}, u32[]{:S(2)}) collective-permute-start(f32[64,192]{1,0:T(8,128)} %get-tuple-element.3), channel_id=1, source_target_pairs={{8,0},{16,8},{24,16},{32,24},{40,32},{48,40},{56,48},{64,56},{72,6... | collective-permute-start | bytes 147464 | tf_op jit(solution)/shard_map/ppermute | solution.py:16
  20.4 10.7 %collective-permute-start.7 = (f32[64,192]{1,0:T(8,128)S(1)}, f32[64,192]{1,0:T(8,128)S(1)}, u32[]{:S(2)}, u32[]{:S(2)}) collective-permute-start(f32[64,192]{1,0:T(8,128)S(1)} %get-tuple-element.9), channel_id=1, source_target_pairs={{32,0},{40,8},{48,16},{56,24},{64,32},{72,40},{80,48},{88,56},{96,... | collective-permute-start | bytes 147464 | tf_op jit(solution)/shard_map/ppermute | solution.py:16
  26.0 13.9 %collective-permute-start.2 = (f32[64,192]{1,0:T(8,128)}, f32[64,192]{1,0:T(8,128)}, u32[]{:S(2)}, u32[]{:S(2)}) collective-permute-start(f32[64,192]{1,0:T(8,128)} %get-tuple-element.4), channel_id=1, source_target_pairs={{240,0},{248,8},{0,16},{8,24},{16,32},{24,40},{32,48},{40,56},{48,... | collective-permute-start | bytes 147464 | tf_op jit(solution)/shard_map/ppermute | solution.py:16
  68.6 41.9 %collective-permute-start.8 = (f32[64,192]{1,0:T(8,128)S(1)}, f32[64,192]{1,0:T(8,128)S(1)}, u32[]{:S(2)}, u32[]{:S(2)}) collective-permute-start(f32[64,192]{1,0:T(8,128)S(1)} %get-tuple-element.34), channel_id=1, source_target_pairs={{248,0},{0,8},{8,16},{16,24},{24,32},{32,40},{40,48},{48,56},{56,6... | collective-permute-start | bytes 147464 | tf_op jit(solution)/shard_map/ppermute | solution.py:16
  68.7 39.0 %collective-permute-start.15 = (f32[64,192]{1,0:T(8,128)S(1)}, f32[64,192]{1,0:T(8,128)S(1)}, u32[]{:S(2)}, u32[]{:S(2)}) collective-permute-start(f32[64,192]{1,0:T(8,128)S(1)} %get-tuple-element.35), channel_id=1, source_target_pairs={{32,0},{40,8},{48,16},{56,24},{64,32},{72,40},{80,48},{88,56},{96,... | collective-permute-start | bytes 147464 | tf_op jit(solution)/shard_map/ppermute | solution.py:16
  68.8 35.2 %collective-permute-start.14 = (f32[64,192]{1,0:T(8,128)S(1)}, f32[64,192]{1,0:T(8,128)}, u32[]{:S(2)}, u32[]{:S(2)}) collective-permute-start(f32[64,192]{1,0:T(8,128)S(1)} %get-tuple-element.36), channel_id=1, source_target_pairs={{224,0},{232,8},{240,16},{248,24},{0,32},{8,40},{16,48},{24,56},{3... | collective-permute-start | bytes 147464 | tf_op jit(solution)/shard_map/ppermute | solution.py:16
  71.9 28.5 %collective-permute-start.13 = (f32[64,192]{1,0:T(8,128)S(1)}, f32[64,192]{1,0:T(8,128)}, u32[]{:S(2)}, u32[]{:S(2)}) collective-permute-start(f32[64,192]{1,0:T(8,128)S(1)} %get-tuple-element.37), channel_id=1, source_target_pairs={{24,0},{32,8},{40,16},{48,24},{56,32},{64,40},{72,48},{80,56},{88,... | collective-permute-start | bytes 147464 | tf_op jit(solution)/shard_map/ppermute | solution.py:16
  73.5 23.3 %collective-permute-start.12 = (f32[64,192]{1,0:T(8,128)S(1)}, f32[64,192]{1,0:T(8,128)}, u32[]{:S(2)}, u32[]{:S(2)}) collective-permute-start(f32[64,192]{1,0:T(8,128)S(1)} %get-tuple-element.38), channel_id=1, source_target_pairs={{232,0},{240,8},{248,16},{0,24},{8,32},{16,40},{24,48},{32,56},{40... | collective-permute-start | bytes 147464 | tf_op jit(solution)/shard_map/ppermute | solution.py:16
  76.5 42.9 %all-to-all-start.1 = ((s32[8,48,1]{1,2,0:T(1,128)}), s32[8,48,1]{1,2,0:T(1,128)}, u32[]{:S(2)}, u32[]{:S(2)}) async-start(s32[8,48,1]{1,2,0:T(1,128)} %bitcast.111), calls=%async_computation.1 | async-start | bytes 8192 | tf_op jit(solution)/shard_map/all_to_all | solution.py:77
  119.4 9.9 %all-to-all-start = ((f32[8,1,3072]{2,1,0:T(1,128)}), f32[8,1,3072]{2,1,0:T(1,128)}, u32[]{:S(2)}, u32[]{:S(2)}) async-start(f32[8,1,3072]{2,1,0:T(1,128)} %reshape.668), calls=%async_computation | async-start | bytes 196608 | tf_op jit(solution)/shard_map/all_to_all | solution.py:106
  124.2 150.4 %all-reduce.4.cloned.1.call-start = ((), (), s32[]{:S(2)}) async-start(), calls=%async_computation.5 | async-start | bytes 524288 | tf_op jit(solution)/shard_map/psum | solution.py:110
  136.3 596.3 %all-reduce.6.cloned.1.call-start = ((), (), s32[]{:S(2)}) async-start(), calls=%async_computation.6 | async-start | bytes 524288 | tf_op jit(solution)/shard_map/psum | solution.py:110
  357.3 11.3 %collective-permute-start.19 = (f32[64,192]{1,0:T(8,128)S(1)}, f32[64,192]{1,0:T(8,128)}, u32[]{:S(2)}, u32[]{:S(2)}) collective-permute-start(f32[64,192]{1,0:T(8,128)S(1)} %get-tuple-element.31), channel_id=1, source_target_pairs={{16,0},{24,8},{32,16},{40,24},{48,32},{56,40},{64,48},{72,56},{80,... | collective-permute-start | bytes 147464 | tf_op jit(solution)/shard_map/ppermute | solution.py:16
  360.2 11.0 %collective-permute-start.17 = (f32[64,192]{1,0:T(8,128)S(1)}, f32[64,192]{1,0:T(8,128)}, u32[]{:S(2)}, u32[]{:S(2)}) collective-permute-start(f32[64,192]{1,0:T(8,128)S(1)} %get-tuple-element.33), channel_id=1, source_target_pairs={{8,0},{16,8},{24,16},{32,24},{40,32},{48,40},{56,48},{64,56},{72,6... | collective-permute-start | bytes 147464 | tf_op jit(solution)/shard_map/ppermute | solution.py:16
  364.7 20.5 %collective-permute-start.20 = (f32[64,192]{1,0:T(8,128)}, f32[64,192]{1,0:T(8,128)}, u32[]{:S(2)}, u32[]{:S(2)}) collective-permute-start(f32[64,192]{1,0:T(8,128)} %get-tuple-element.30), channel_id=1, source_target_pairs={{232,0},{240,8},{248,16},{0,24},{8,32},{16,40},{24,48},{32,56},{40... | collective-permute-start | bytes 147464 | tf_op jit(solution)/shard_map/ppermute | solution.py:16
  364.7 22.3 %collective-permute-start.21 = (f32[64,192]{1,0:T(8,128)}, f32[64,192]{1,0:T(8,128)}, u32[]{:S(2)}, u32[]{:S(2)}) collective-permute-start(f32[64,192]{1,0:T(8,128)} %get-tuple-element.29), channel_id=1, source_target_pairs={{24,0},{32,8},{40,16},{48,24},{56,32},{64,40},{72,48},{80,56},{88,... | collective-permute-start | bytes 147464 | tf_op jit(solution)/shard_map/ppermute | solution.py:16
  368.5 20.4 %collective-permute-start.22 = (f32[64,192]{1,0:T(8,128)}, f32[64,192]{1,0:T(8,128)}, u32[]{:S(2)}, u32[]{:S(2)}) collective-permute-start(f32[64,192]{1,0:T(8,128)} %get-tuple-element.28), channel_id=1, source_target_pairs={{224,0},{232,8},{240,16},{248,24},{0,32},{8,40},{16,48},{24,56},{3... | collective-permute-start | bytes 147464 | tf_op jit(solution)/shard_map/ppermute | solution.py:16
  368.5 22.2 %collective-permute-start.23 = (f32[64,192]{1,0:T(8,128)}, f32[64,192]{1,0:T(8,128)}, u32[]{:S(2)}, u32[]{:S(2)}) collective-permute-start(f32[64,192]{1,0:T(8,128)} %get-tuple-element.27), channel_id=1, source_target_pairs={{32,0},{40,8},{48,16},{56,24},{64,32},{72,40},{80,48},{88,56},{96,... | collective-permute-start | bytes 147464 | tf_op jit(solution)/shard_map/ppermute | solution.py:16
  371.2 21.3 %collective-permute-start.16 = (f32[64,192]{1,0:T(8,128)}, f32[64,192]{1,0:T(8,128)}, u32[]{:S(2)}, u32[]{:S(2)}) collective-permute-start(f32[64,192]{1,0:T(8,128)} %get-tuple-element.26), channel_id=1, source_target_pairs={{248,0},{0,8},{8,16},{16,24},{24,32},{32,40},{40,48},{48,56},{56,6... | collective-permute-start | bytes 147464 | tf_op jit(solution)/shard_map/ppermute | solution.py:16
  804.3 11.0 %collective-permute-start.35 = (f32[64,192]{1,0:T(8,128)S(1)}, f32[64,192]{1,0:T(8,128)S(1)}, u32[]{:S(2)}, u32[]{:S(2)}) collective-permute-start(f32[64,192]{1,0:T(8,128)S(1)} %get-tuple-element.15), channel_id=1, source_target_pairs={{16,0},{24,8},{32,16},{40,24},{48,32},{56,40},{64,48},{72,56},{80,... | collective-permute-start | bytes 147464 | tf_op jit(solution)/shard_map/ppermute | solution.py:16
  807.2 10.8 %collective-permute-start.33 = (f32[64,192]{1,0:T(8,128)S(1)}, f32[64,192]{1,0:T(8,128)S(1)}, u32[]{:S(2)}, u32[]{:S(2)}) collective-permute-start(f32[64,192]{1,0:T(8,128)S(1)} %get-tuple-element.17), channel_id=1, source_target_pairs={{8,0},{16,8},{24,16},{32,24},{40,32},{48,40},{56,48},{64,56},{72,6... | collective-permute-start | bytes 147464 | tf_op jit(solution)/shard_map/ppermute | solution.py:16
  811.7 10.3 %collective-permute-start.37 = (f32[64,192]{1,0:T(8,128)}, f32[64,192]{1,0:T(8,128)}, u32[]{:S(2)}, u32[]{:S(2)}) collective-permute-start(f32[64,192]{1,0:T(8,128)} %get-tuple-element.13), channel_id=1, source_target_pairs={{24,0},{32,8},{40,16},{48,24},{56,32},{64,40},{72,48},{80,56},{88,... | collective-permute-start | bytes 147464 | tf_op jit(solution)/shard_map/ppermute | solution.py:16
  815.3 10.3 %collective-permute-start.39 = (f32[64,192]{1,0:T(8,128)S(1)}, f32[64,192]{1,0:T(8,128)}, u32[]{:S(2)}, u32[]{:S(2)}) collective-permute-start(f32[64,192]{1,0:T(8,128)S(1)} %get-tuple-element.11), channel_id=1, source_target_pairs={{32,0},{40,8},{48,16},{56,24},{64,32},{72,40},{80,48},{88,56},{96,... | collective-permute-start | bytes 147464 | tf_op jit(solution)/shard_map/ppermute | solution.py:16
  (76 other events, 2504.3 us)
Sparse Core Ops, SparseCore 0:
  136.4 138.1 all-reduce.3
  596.4 136.1 all-reduce.5
where the time goes:
time: 927 us; the launch traced here: 918 us
  blocking collectives  366 us (39%)
  waiting for transfers between devices  278 us (30%)
  local copies, waits for them, and re-layouts  105 us (11%)
  starting transfers between devices  83.3 us (9%)
  other arithmetic  39.7 us (4%)
  matrix products  30.5 us (3%)
  between operations  15.6 us (2%)
    psum x2, waiting for transfers between devices, shards(): coarse_rhs = lax.psum(gathered, 'sub')  275 us
    psum x2, blocking collectives, residual_norm(): return lax.psum(jnp.sum(first * second, axis=1), ('sub', 'agg'))  155 us
    psum x1, blocking collectives, shards(): lax.psum(jnp.sum(direction * image, axis=1), ('sub', 'agg'))  77.7 us
    all_gather x2, blocking collectives, shards(): coarse_sol = lax.all_gather(partial_rows, 'sub', axis=1, tiled=True)  71.7 us
    ppermute x40, starting transfers between devices, from_behind_2(): return lax.ppermute(block, axis, route)  68.3 us
    all_to_all x2, blocking collectives, shards(): lax.all_to_all(answer, 'agg', split_axis=1, concat_axis=1, tiled=True)  53.4 us
    mul x52, local copies, waits for them, and re-layouts, assemble(): to_behind * from_behind[:, None, :]  46.7 us
    mul x44, local copies, waits for them, and re-layouts, assemble(): to_ahead * from_ahead[:, None, :]  40.9 us
  transfers between devices with their start and end apart: 44, of which 4 were waited for; matrix products, arithmetic and copies ran while one was open for 10% of the time, Pallas kernels for 0%

commit v1 on v0

--- a/solution.py
+++ b/solution.py
@@ -8,6 +8,10 @@
 ITERS = 2
 FULL_PRECISION = lax.Precision.HIGHEST
 CONTRACT_LAST = (((1,), (1,)), ((), ()))
+
+
+def _match_words(inner_x):
+    return lax.all_gather(inner_x, ("sub", "agg")).sum(axis=0)
 
 
 def from_behind_2(block, axis, distance):
@@ -121,9 +125,7 @@
             local_back.astype(jnp.bfloat16), coupling_block, preferred_element_type=jnp.float32
         )
         image = assemble(inside * (own + correction))
-        alpha = (residual_dot / lax.psum(jnp.sum(direction * image, axis=1), ("sub", "agg")))[
-            :, None
-        ]
+        alpha = (residual_dot / _match_words(jnp.sum(direction * image, axis=1)))[:, None]
         solution = solution + alpha * direction
         residual = residual - alpha * image
         if iteration + 1 < ITERS:

time: 927 us -> 1260 us (1.36)
  waiting for transfers between devices: 278 us -> 682 us
  blocking collectives: 366 us -> 289 us
    unnamed x2 -> x6, waiting for transfers between devices: 0.03 us -> 404 us
    psum x1 -> x0, blocking collectives: 77.7 us -> none  [shards(): lax.psum(jnp.sum(direction * image, axis=1), ('sub', 'agg'))]
  transfers between devices with their start and end apart: 44 -> 46, of which waited for: 4 -> 6; matrix products, arithmetic and copies ran while one was open for 10% -> 8% of each run, Pallas kernels for 0% -> 0%
where the time goes in v1:
time: 1260 us; the launch traced here: 1250 us
  waiting for transfers between devices  682 us (54%)
  blocking collectives  289 us (23%)
  local copies, waits for them, and re-layouts  109 us (9%)
  starting transfers between devices  84.7 us (7%)
  other arithmetic  39.2 us (3%)
  matrix products  30.6 us (2%)
  between operations  15.4 us (1%)
    unnamed x6, waiting for transfers between devices  404 us
    psum x2, waiting for transfers between devices, shards(): coarse_rhs = lax.psum(gathered, 'sub')  275 us
    psum x2, blocking collectives, residual_norm(): return lax.psum(jnp.sum(first * second, axis=1), ('sub', 'agg'))  156 us
    all_gather x2, blocking collectives, shards(): coarse_sol = lax.all_gather(partial_rows, 'sub', axis=1, tiled=True)  71.7 us
    ppermute x40, starting transfers between devices, from_behind_2(): return lax.ppermute(block, axis, route)  69.6 us
    all_to_all x2, blocking collectives, shards(): lax.all_to_all(answer, 'agg', split_axis=1, concat_axis=1, tiled=True)  53.4 us
    mul x52, local copies, waits for them, and re-layouts, assemble(): to_behind * from_behind[:, None, :]  46.7 us
    mul x44, local copies, waits for them, and re-layouts, assemble(): to_ahead * from_ahead[:, None, :]  40.9 us
  transfers between devices with their start and end apart: 46, of which 6 were waited for; matrix products, arithmetic and copies ran while one was open for 8% of the time, Pallas kernels for 0%

profile of v1, /device:TPU:1, one launch (start us, length us, event | category | flops | bytes accessed | tf_op | source)
XLA Modules:
  0.0 1249.8 jit_solution(7072752203422601458)
XLA Ops:
  13.6 6.6 collective-permute-start.1
  50.9 5.2 fusion.8
  60.5 4.7 collective-permute-start.11
  76.6 10.2 all-to-all-start.1
  119.5 4.8 all-to-all-start
  136.4 138.3 %all-reduce.7.cloned.1.call-done = f32[64,1024]{1,0:T(8,128)} async-done(((f32[64,1024]{1,0:T(8,128)}), f32[64,1024]{1,0:T(8,128)}) %all-reduce.7.cloned.1.call-update) | async-done | bytes 262160 | tf_op jit(solution)/shard_map/psum | solution.py:114
  276.0 35.9 %all_gather.18 = f32[64,1024]{0,1:T(8,128)S(1)} all-gather(f32[64,32]{0,1:T(8,128)S(1)} %fusion.58), channel_id=1, replica_groups=mesh['sub'=32,'agg'=8] {'sub'}, dimensions={1}, use_global_device_ids=true | all-gather | bytes 270336 | tf_op jit(solution)/shard_map/all_gather | solution.py:118
  315.8 26.7 %all_to_all.54 = f32[8,1,3072]{2,1,0:T(1,128)} all-to-all(f32[8,1,3072]{2,1,0:T(1,128)} %reshape.676), channel_id=1, replica_groups=mesh['sub'=32,'agg'=8] {'agg'}, dimensions={0} | all-to-all | bytes 196608 | tf_op jit(solution)/shard_map/all_to_all | solution.py:120
  348.1 4.0 fusion.23
  360.3 4.5 collective-permute-start.17
  364.8 3.8 collective-permute-start.21
  394.5 3.9 multiply_reduce_fusion.42
  399.5 78.1 %psum.28 = f32[64]{0:T(128)S(1)} all-reduce(f32[64]{0:T(128)S(1)} %get-tuple-element.43), channel_id=1, replica_groups=mesh['sub'=32,'agg'=8] {'sub','agg'}, use_global_device_ids=true, to_apply=%region_17.18 | all-reduce | flops 64 | bytes 512 | tf_op jit(solution)/shard_map/psum | solution.py:94
  477.6 162.8 %all-reduce.11.cloned.1.call-done = f32[16384]{0:T(1024)} async-done(((f32[16384]{0:T(1024)}), f32[16384]{0:T(1024)}) %all-reduce.11.cloned.1.call-update) | async-done | bytes 65552
  650.9 3.7 collective-permute-start.25
  654.6 3.6 collective-permute-start.29
  672.5 77.8 %psum.30 = f32[64]{0:T(128)S(1)} all-reduce(f32[64]{0:T(128)S(1)} %get-tuple-element.46), channel_id=1, replica_groups=mesh['sub'=32,'agg'=8] {'sub','agg'}, use_global_device_ids=true, to_apply=%region_41.42 | all-reduce | flops 64 | bytes 512 | tf_op jit(solution)/shard_map/psum | solution.py:94
  752.5 8.5 all_to_all.55
  763.4 137.0 %all-reduce.9.cloned.1.call-done = f32[64,1024]{1,0:T(8,128)} async-done(((f32[64,1024]{1,0:T(8,128)}), f32[64,1024]{1,0:T(8,128)}) %all-reduce.9.cloned.1.call-update) | async-done | bytes 262160 | tf_op jit(solution)/shard_map/psum | solution.py:114
  901.7 35.9 %all_gather.21 = f32[64,1024]{0,1:T(8,128)S(1)} all-gather(f32[64,32]{0,1:T(8,128)S(1)} %fusion.56), channel_id=1, replica_groups=mesh['sub'=32,'agg'=8] {'sub'}, dimensions={1}, use_global_device_ids=true | all-gather | bytes 270336 | tf_op jit(solution)/shard_map/all_gather | solution.py:118
  938.7 26.7 %all_to_all.56 = f32[8,1,3072]{2,1,0:T(1,128)S(1)} all-to-all(f32[8,1,3072]{2,1,0:T(1,128)S(1)} %reshape.680), channel_id=1, replica_groups=mesh['sub'=32,'agg'=8] {'agg'}, dimensions={0} | all-to-all | bytes 196608 | tf_op jit(solution)/shard_map/all_to_all | solution.py:120
  975.1 4.5 collective-permute-start.33
  979.6 3.6 collective-permute-start.37
  1000.0 240.8 %all-reduce.13.cloned.1.call-done = f32[16384]{0:T(1024)} async-done(((f32[16384]{0:T(1024)}), f32[16384]{0:T(1024)}) %all-reduce.13.cloned.1.call-update) | async-done | bytes 65552
  (374 shorter events, 203.0 us)
Async XLA Ops:
  11.5 35.6 %collective-permute-start = (f32[64,192]{1,0:T(8,128)S(1)}, f32[64,192]{1,0:T(8,128)}, u32[]{:S(2)}, u32[]{:S(2)}) collective-permute-start(f32[64,192]{1,0:T(8,128)S(1)} %get-tuple-element.2), channel_id=1, source_target_pairs={{248,0},{0,8},{8,16},{16,24},{24,32},{32,40},{40,48},{48,56},{56,6... | collective-permute-start | bytes 147464 | tf_op jit(solution)/shard_map/ppermute | solution.py:20
  13.6 29.9 %collective-permute-start.1 = (f32[64,192]{1,0:T(8,128)}, f32[64,192]{1,0:T(8,128)}, u32[]{:S(2)}, u32[]{:S(2)}) collective-permute-start(f32[64,192]{1,0:T(8,128)} %get-tuple-element.3), channel_id=1, source_target_pairs={{8,0},{16,8},{24,16},{32,24},{40,32},{48,40},{56,48},{64,56},{72,6... | collective-permute-start | bytes 147464 | tf_op jit(solution)/shard_map/ppermute | solution.py:20
  20.4 10.7 collective-permute-start.7
  26.0 13.9 %collective-permute-start.2 = (f32[64,192]{1,0:T(8,128)}, f32[64,192]{1,0:T(8,128)}, u32[]{:S(2)}, u32[]{:S(2)}) collective-permute-start(f32[64,192]{1,0:T(8,128)} %get-tuple-element.4), channel_id=1, source_target_pairs={{240,0},{248,8},{0,16},{8,24},{16,32},{24,40},{32,48},{40,56},{48,... | collective-permute-start | bytes 147464 | tf_op jit(solution)/shard_map/ppermute | solution.py:20
  68.7 41.9 %collective-permute-start.8 = (f32[64,192]{1,0:T(8,128)S(1)}, f32[64,192]{1,0:T(8,128)S(1)}, u32[]{:S(2)}, u32[]{:S(2)}) collective-permute-start(f32[64,192]{1,0:T(8,128)S(1)} %get-tuple-element.34), channel_id=1, source_target_pairs={{248,0},{0,8},{8,16},{16,24},{24,32},{32,40},{40,48},{48,56},{56,6... | collective-permute-start | bytes 147464 | tf_op jit(solution)/shard_map/ppermute | solution.py:20
  68.8 39.0 %collective-permute-start.15 = (f32[64,192]{1,0:T(8,128)S(1)}, f32[64,192]{1,0:T(8,128)S(1)}, u32[]{:S(2)}, u32[]{:S(2)}) collective-permute-start(f32[64,192]{1,0:T(8,128)S(1)} %get-tuple-element.35), channel_id=1, source_target_pairs={{32,0},{40,8},{48,16},{56,24},{64,32},{72,40},{80,48},{88,56},{96,... | collective-permute-start | bytes 147464 | tf_op jit(solution)/shard_map/ppermute | solution.py:20
  68.9 35.2 %collective-permute-start.14 = (f32[64,192]{1,0:T(8,128)S(1)}, f32[64,192]{1,0:T(8,128)}, u32[]{:S(2)}, u32[]{:S(2)}) collective-permute-start(f32[64,192]{1,0:T(8,128)S(1)} %get-tuple-element.36), channel_id=1, source_target_pairs={{224,0},{232,8},{240,16},{248,24},{0,32},{8,40},{16,48},{24,56},{3... | collective-permute-start | bytes 147464 | tf_op jit(solution)/shard_map/ppermute | solution.py:20
  72.0 28.5 %collective-permute-start.13 = (f32[64,192]{1,0:T(8,128)S(1)}, f32[64,192]{1,0:T(8,128)}, u32[]{:S(2)}, u32[]{:S(2)}) collective-permute-start(f32[64,192]{1,0:T(8,128)S(1)} %get-tuple-element.37), channel_id=1, source_target_pairs={{24,0},{32,8},{40,16},{48,24},{56,32},{64,40},{72,48},{80,56},{88,... | collective-permute-start | bytes 147464 | tf_op jit(solution)/shard_map/ppermute | solution.py:20
  73.5 23.3 %collective-permute-start.12 = (f32[64,192]{1,0:T(8,128)S(1)}, f32[64,192]{1,0:T(8,128)}, u32[]{:S(2)}, u32[]{:S(2)}) collective-permute-start(f32[64,192]{1,0:T(8,128)S(1)} %get-tuple-element.38), channel_id=1, source_target_pairs={{232,0},{240,8},{248,16},{0,24},{8,32},{16,40},{24,48},{32,56},{40... | collective-permute-start | bytes 147464 | tf_op jit(solution)/shard_map/ppermute | solution.py:20
  76.6 42.9 %all-to-all-start.1 = ((s32[8,48,1]{1,2,0:T(1,128)}), s32[8,48,1]{1,2,0:T(1,128)}, u32[]{:S(2)}, u32[]{:S(2)}) async-start(s32[8,48,1]{1,2,0:T(1,128)} %bitcast.111), calls=%async_computation.1 | async-start | bytes 8192 | tf_op jit(solution)/shard_map/all_to_all | solution.py:81
  124.3 150.4 %all-reduce.7.cloned.1.call-start = ((), (), s32[]{:S(2)}) async-start(), calls=%async_computation.5 | async-start | bytes 524288 | tf_op jit(solution)/shard_map/psum | solution.py:114
  136.3 504.1 %all-reduce.11.cloned.1.call-start = ((), (), s32[]{:S(2)}) async-start(), calls=%async_computation.7 | async-start | bytes 131072
  357.3 11.3 collective-permute-start.19
  360.3 11.0 collective-permute-start.17
  364.8 20.5 %collective-permute-start.20 = (f32[64,192]{1,0:T(8,128)}, f32[64,192]{1,0:T(8,128)}, u32[]{:S(2)}, u32[]{:S(2)}) collective-permute-start(f32[64,192]{1,0:T(8,128)} %get-tuple-element.30), channel_id=1, source_target_pairs={{232,0},{240,8},{248,16},{0,24},{8,32},{16,40},{24,48},{32,56},{40... | collective-permute-start | bytes 147464 | tf_op jit(solution)/shard_map/ppermute | solution.py:20
  364.8 22.3 %collective-permute-start.21 = (f32[64,192]{1,0:T(8,128)}, f32[64,192]{1,0:T(8,128)}, u32[]{:S(2)}, u32[]{:S(2)}) collective-permute-start(f32[64,192]{1,0:T(8,128)} %get-tuple-element.29), channel_id=1, source_target_pairs={{24,0},{32,8},{40,16},{48,24},{56,32},{64,40},{72,48},{80,56},{88,... | collective-permute-start | bytes 147464 | tf_op jit(solution)/shard_map/ppermute | solution.py:20
  368.6 20.4 %collective-permute-start.22 = (f32[64,192]{1,0:T(8,128)}, f32[64,192]{1,0:T(8,128)}, u32[]{:S(2)}, u32[]{:S(2)}) collective-permute-start(f32[64,192]{1,0:T(8,128)} %get-tuple-element.28), channel_id=1, source_target_pairs={{224,0},{232,8},{240,16},{248,24},{0,32},{8,40},{16,48},{24,56},{3... | collective-permute-start | bytes 147464 | tf_op jit(solution)/shard_map/ppermute | solution.py:20
  368.6 22.2 %collective-permute-start.23 = (f32[64,192]{1,0:T(8,128)}, f32[64,192]{1,0:T(8,128)}, u32[]{:S(2)}, u32[]{:S(2)}) collective-permute-start(f32[64,192]{1,0:T(8,128)} %get-tuple-element.27), channel_id=1, source_target_pairs={{32,0},{40,8},{48,16},{56,24},{64,32},{72,40},{80,48},{88,56},{96,... | collective-permute-start | bytes 147464 | tf_op jit(solution)/shard_map/ppermute | solution.py:20
  371.3 21.3 %collective-permute-start.16 = (f32[64,192]{1,0:T(8,128)}, f32[64,192]{1,0:T(8,128)}, u32[]{:S(2)}, u32[]{:S(2)}) collective-permute-start(f32[64,192]{1,0:T(8,128)} %get-tuple-element.26), channel_id=1, source_target_pairs={{248,0},{0,8},{8,16},{16,24},{24,32},{32,40},{40,48},{48,56},{56,6... | collective-permute-start | bytes 147464 | tf_op jit(solution)/shard_map/ppermute | solution.py:20
  399.5 500.9 %all-reduce.9.cloned.1.call-start = ((), (), s32[]{:S(2)}) async-start(), calls=%async_computation.6 | async-start | bytes 524288 | tf_op jit(solution)/shard_map/psum | solution.py:114
  763.4 477.4 %all-reduce.13.cloned.1.call-start = ((), (), s32[]{:S(2)}) async-start(), calls=%async_computation.8 | async-start | bytes 131072
  972.1 11.0 collective-permute-start.35
  975.1 10.8 collective-permute-start.33
  983.2 10.3 collective-permute-start.39
  (81 other events, 4434.6 us)
Sparse Core Ops, SparseCore 0:
  136.5 138.1 all-reduce.6
  399.6 240.7 all-reduce.10
  763.5 136.8 all-reduce.8
  1000.2 240.6 all-reduce.12
